TPU v7x, 32 devices: a whole 2x2x4 slice. The times are simulated.
32 devices in a mesh: prow: 8 (over z, x), pcol: 4 (over y, core).
Axes of the slice: x: 2, y: 2, z: 4, core: 2. Of those that a mesh axis runs over, the one named last changes fastest.
Arguments:
- sigma_top: bfloat16 [8, 8, 128, 128], P('prow', 'pcol'), may hold values from -6 to 6
- factor_one: bfloat16 [8, 8, 128, 128], P('prow', 'pcol'), may hold values from -0.1875 to 0.1875
- inverse_one: bfloat16 [8, 128, 128], P('prow'), may hold values from -0.5 to 0.5
- pattern_one: int32 [8, 8], replicated, may hold values from 0 to 7, as said below
- factor_two: bfloat16 [8, 8, 128, 128], P('prow', 'pcol'), may hold values from -0.25 to 0.25
- parent_block: bfloat16 [8, 128, 128], P('prow'), may hold values from -0.25 to 0.25
- inverse_two: bfloat16 [8, 128, 128], P('prow'), may hold values from -0.5 to 0.5
- parent_two: int32 [8], replicated, may hold values from 0 to 7
- keep_two: int32 [8, 8], replicated, may hold values 0 or 1
Outputs:
- inverse_top_one: bfloat16 [8, 8, 128, 128], P('prow')
- diag_one: float32 [8, 128, 128], P('prow')
- inverse_top_two: bfloat16 [8, 8, 128, 128], P('prow')
- inverse_parent_two: float32 [8, 128, 128], P('prow')
- diag_two: float32 [8, 128, 128], P('prow')
Inputs may be any that keep to these rules, and one draw needn't show every extreme that they name: Each row of pattern_one lists 8 distinct block rows of the top region. keep_two[i, k] = 1 where level-two supernode i's pattern holds the k-th tile of its parent's pattern. parent_two names level-one supernodes.
All inputs are finite; a program needn't handle non-finite values.
Results may differ from a plain program's by a relative error of at most 0.023.
Values may be sent and summed in bfloat16 or wider, within the bound.
A program may use at most 64 MiB of HBM per device.

v0:
```python
import jax
import jax.numpy as jnp
from jax import lax
from jax.sharding import PartitionSpec as P

highest = lax.Precision.HIGHEST


def split_product(form, left, right):
    upper_part = right.astype(jnp.bfloat16)
    lower_part = (right - upper_part.astype(jnp.float32)).astype(jnp.bfloat16)
    first = jnp.einsum(form, left, upper_part, preferred_element_type=jnp.float32)
    return first + jnp.einsum(form, left, lower_part, preferred_element_type=jnp.float32)


def body(
    sigma_top,
    factor_one,
    inverse_one,
    pattern_one,
    factor_two,
    parent_block,
    inverse_two,
    parent_two,
    keep_two,
):
    rows_here = sigma_top.shape[0]
    cols_here = sigma_top.shape[1]
    tile_width = sigma_top.shape[2]
    prow_index = lax.axis_index("prow")
    pcol_index = lax.axis_index("pcol")
    first_row = prow_index * rows_here
    column_ids = pcol_index * cols_here + jnp.arange(cols_here, dtype=jnp.int32)
    top_rows = first_row + jnp.arange(rows_here, dtype=jnp.int32)
    owner_column = first_row // cols_here
    diagonal_owner = owner_column == pcol_index
    offset = jnp.clip(first_row - pcol_index * cols_here, 0, cols_here - rows_here)
    total_one = pattern_one.shape[0]
    local_one = factor_one.shape[0]
    lower_one = jnp.tril(inverse_one)
    scaled_local = jnp.einsum(
        "jkwv,jvx->jkwx", factor_one, lower_one, preferred_element_type=jnp.float32
    ).astype(jnp.bfloat16)
    scaled_rows = lax.all_gather(scaled_local, "pcol", axis=1, tiled=True)
    own_pattern = lax.dynamic_slice_in_dim(pattern_one, prow_index * local_one, local_one, 0)
    picker_one = (own_pattern[:, :, None] == column_ids[None, None, :]).astype(jnp.bfloat16)
    spread_one = jnp.einsum(
        "jkc,jkwv->jcwv", picker_one, scaled_rows, preferred_element_type=jnp.float32
    ).astype(jnp.bfloat16)
    spread_all = lax.all_gather(spread_one, "prow", axis=0, tiled=True)
    partial_one = jnp.einsum(
        "acwv,jcvx->ajwx", sigma_top, spread_all, preferred_element_type=jnp.float32
    )
    summed_one = lax.psum(partial_one.astype(jnp.bfloat16), "pcol").astype(jnp.float32)
    member_one = jnp.sum(
        (pattern_one[None, :, :] == top_rows[:, None, None]).astype(jnp.float32), axis=2
    )
    inverse_top_one = (-summed_one * member_one[:, :, None, None]).astype(jnp.bfloat16)
    own_rows = lax.dynamic_slice_in_dim(spread_all, offset, rows_here, 1)
    quadratic_one = split_product("jawv,ajwx->jvx", own_rows, summed_one)
    quadratic_one = jnp.where(diagonal_owner, quadratic_one, 0.0)
    lower_float = lower_one.astype(jnp.float32)
    gram_one = jnp.einsum("jwv,jwx->jvx", lower_float, lower_float, precision=highest)
    placed = lax.dynamic_update_slice_in_dim(
        jnp.zeros((total_one, tile_width, tile_width), jnp.float32),
        gram_one,
        prow_index * local_one,
        0,
    )
    partial_diag = quadratic_one + jnp.where(pcol_index == 0, placed, 0.0)
    diagonal_all = lax.psum(partial_diag, ("prow", "pcol"))
    diag_one = lax.dynamic_slice_in_dim(diagonal_all, prow_index * local_one, local_one, 0)
    local_two = factor_two.shape[0]
    lower_two = jnp.tril(inverse_two)
    scaled_two = jnp.einsum(
        "ikwv,ivx->ikwx", factor_two, lower_two, preferred_element_type=jnp.float32
    ).astype(jnp.bfloat16)
    scaled_parent = jnp.einsum(
        "iwv,ivx->iwx", parent_block, lower_two, preferred_element_type=jnp.float32
    ).astype(jnp.bfloat16)
    scaled_rows_two = lax.all_gather(scaled_two, "pcol", axis=1, tiled=True)
    parent_hot = (parent_two[:, None] == jnp.arange(total_one, dtype=jnp.int32)[None, :]).astype(
        jnp.int32
    )
    parent_pattern = jnp.sum(parent_hot[:, :, None] * pattern_one[None, :, :], axis=1)
    own_parent_pattern = lax.dynamic_slice_in_dim(
        parent_pattern, prow_index * local_two, local_two, 0
    )
    own_keep = lax.dynamic_slice_in_dim(keep_two, prow_index * local_two, local_two, 0)
    picker_two = (
        (own_parent_pattern[:, :, None] == column_ids[None, None, :]).astype(jnp.int32)
        * own_keep[:, :, None]
    ).astype(jnp.bfloat16)
    spread_two = jnp.einsum(
        "ikc,ikwv->icwv", picker_two, scaled_rows_two, preferred_element_type=jnp.float32
    ).astype(jnp.bfloat16)
    spread_all_two, parent_all = (
        lax.all_gather(spread_two, "prow", axis=0, tiled=True),
        lax.all_gather(scaled_parent, "prow", axis=0, tiled=True),
    )
    partial_two = jnp.einsum(
        "acwv,icvx->aiwx", sigma_top, spread_all_two, preferred_element_type=jnp.float32
    )
    inherited = jnp.einsum(
        "ij,ajwv->aiwv",
        parent_hot.astype(jnp.bfloat16),
        inverse_top_one,
        preferred_element_type=jnp.float32,
    ).astype(jnp.bfloat16)
    carried_rows = jnp.einsum(
        "aiwv,ivx->aiwx", inherited, parent_all, preferred_element_type=jnp.float32
    )
    partial_two = partial_two + jnp.where(diagonal_owner, carried_rows, 0.0)
    summed_two = lax.psum(partial_two.astype(jnp.bfloat16), "pcol").astype(jnp.float32)
    member_two = jnp.sum(
        (parent_pattern[None, :, :] == top_rows[:, None, None]).astype(jnp.float32)
        * keep_two[None, :, :].astype(jnp.float32),
        axis=2,
    )
    inverse_top_two = (-summed_two * member_two[:, :, None, None]).astype(jnp.bfloat16)
    own_two = lax.dynamic_slice_in_dim(spread_all_two, offset, rows_here, 1)
    cross = jnp.einsum("aiwv,iawx->ivx", inherited, own_two, preferred_element_type=jnp.float32)
    quadratic_two = split_product("iawv,aiwx->ivx", own_two, summed_two)
    cross = jnp.where(diagonal_owner, cross, 0.0)
    quadratic_two = jnp.where(diagonal_owner, quadratic_two, 0.0)
    cross_part, quadratic_part = (
        lax.psum_scatter(
            cross.astype(jnp.bfloat16), "prow", scatter_dimension=0, tiled=True
        ).astype(jnp.float32),
        lax.psum_scatter(
            quadratic_two.astype(jnp.bfloat16), "prow", scatter_dimension=0, tiled=True
        ).astype(jnp.float32),
    )
    cross_sum, quadratic_sum = (
        lax.psum(cross_part.astype(jnp.bfloat16), "pcol").astype(jnp.float32),
        lax.psum(quadratic_part.astype(jnp.bfloat16), "pcol").astype(jnp.float32),
    )
    own_hot = lax.dynamic_slice_in_dim(parent_hot, prow_index * local_two, local_two, 0).astype(
        jnp.float32
    )
    parent_diag = jnp.einsum("ij,jwv->iwv", own_hot, diagonal_all, precision=highest)
    parent_float = scaled_parent.astype(jnp.float32)
    carried = cross_sum + jnp.einsum("iwv,ivx->iwx", parent_diag, parent_float, precision=highest)
    lower_two_float = lower_two.astype(jnp.float32)
    diag_two = jnp.einsum("iwv,iwx->ivx", lower_two_float, lower_two_float, precision=highest)
    diag_two = (
        diag_two
        + quadratic_sum
        + jnp.einsum("iwv,iwx->ivx", parent_float, carried, precision=highest)
    )
    return (inverse_top_one, diag_one, inverse_top_two, -carried, diag_two)


def solution(mesh):
    in_specs = (
        P("prow", "pcol", None, None),
        P("prow", "pcol", None, None),
        P("prow", None, None),
        P(),
        P("prow", "pcol", None, None),
        P("prow", None, None),
        P("prow", None, None),
        P(),
        P(),
    )
    out_specs = (
        P("prow", None, None, None),
        P("prow", None, None),
        P("prow", None, None, None),
        P("prow", None, None),
        P("prow", None, None),
    )
    return jax.shard_map(body, mesh=mesh, in_specs=in_specs, out_specs=out_specs, check_vma=False)
```

profile of v0, /device:TPU:0, one launch (start us, length us, event | category | flops | bytes accessed | tf_op | source)
XLA Modules:
  0.0 453.0 jit_solution(8151209483114322396)
XLA Ops:
  7.2 1.1 fusion.10
  8.4 7.2 %all-gather = bf16[8,128,128]{2,1,0:T(8,128)(2,1)S(1)} all-gather(bf16[2,128,128]{2,1,0:T(8,128)(2,1)S(1)} %copy.72), channel_id=2, replica_groups=mesh['prow'=8,'pcol'=4] {'pcol'}, dimensions={0}, use_global_device_ids=true | all-gather | bytes 327680 | tf_op jit(solution)/shard_map/all_gather | solution.py:44
  16.0 31.9 %all-gather.1 = bf16[16,128,128]{2,1,0:T(8,128)(2,1)S(1)} all-gather(bf16[2,128,128]{2,1,0:T(8,128)(2,1)S(1)} %copy.74), channel_id=3, replica_groups=mesh['prow'=8,'pcol'=4] {'prow'}, dimensions={0}, use_global_device_ids=true | all-gather | bytes 589824 | tf_op jit(solution)/shard_map/all_gather | solution.py:50
  47.9 1.1 fusion.7
  49.5 0.3 copy-done.11
  50.0 0.6 copy-done.10
  50.9 5.8 %all-gather.2 = bf16[8,128,128]{2,1,0:T(8,128)(2,1)S(1)} all-gather(bf16[2,128,128]{2,1,0:T(8,128)(2,1)S(1)} %copy.79), channel_id=4, replica_groups=mesh['prow'=8,'pcol'=4] {'pcol'}, dimensions={0}, use_global_device_ids=true | all-gather | bytes 327680 | tf_op jit(solution)/shard_map/all_gather | solution.py:81
  57.0 31.5 %all-gather.3 = bf16[16,128,128]{2,1,0:T(8,128)(2,1)S(1)} all-gather(bf16[2,128,128]{2,1,0:T(8,128)(2,1)S(1)} %copy.81), channel_id=5, replica_groups=mesh['prow'=8,'pcol'=4] {'prow'}, dimensions={0}, use_global_device_ids=true | all-gather | bytes 589824 | tf_op jit(solution)/shard_map/all_gather | solution.py:98
  88.7 26.4 %all-gather.4 = bf16[1024,128]{0,1:T(8,128)(2,1)S(1)} all-gather(bf16[128,128]{0,1:T(8,128)(2,1)S(1)} %bitcast.162), channel_id=6, replica_groups=mesh['prow'=8,'pcol'=4] {'prow'}, dimensions={0}, use_global_device_ids=true | all-gather | bytes 294912 | tf_op jit(solution)/shard_map/all_gather | solution.py:99
  115.1 0.3 convolution_bitcast_fusion
  115.5 1.1 fusion.112
  117.2 0.9 fusion.9
  118.2 0.9 copy-done.1
  119.1 0.3 fusion.37
  119.4 0.3 fusion.2
  119.7 0.4 copy-done.5
  120.4 0.8 copy-done.2
  121.5 1.0 fusion.6
  122.7 26.8 %all-reduce.10.cloned.1.call-done = bf16[1,8,128,128]{2,3,1,0:T(8,128)(2,1)} async-done(((bf16[1,8,128,128]{2,3,1,0:T(8,128)(2,1)}), bf16[1,8,128,128]{2,3,1,0:T(8,128)(2,1)}) %all-reduce.10.cloned.1.call-update) | async-done | bytes 262160 | tf_op jit(solution)/shard_map/psum | solution.py:114
  149.5 1.3 fusion.32
  150.9 1.0 fusion.3
  152.1 0.9 copy.92
  153.0 0.9 copy.93
  153.9 128.7 %all-reduce.8.cloned.1.call-done = f32[8,128,128]{2,1,0:T(8,128)} async-done(((f32[8,128,128]{2,1,0:T(8,128)}), f32[8,128,128]{2,1,0:T(8,128)}) %all-reduce.8.cloned.1.call-update) | async-done | bytes 524304 | tf_op jit(solution)/shard_map/psum | solution.py:71
  282.6 1.8 fusion.24
  284.5 61.9 %reduce-scatter.3.cloned.1.call-done = bf16[1,128,128]{2,1,0:T(8,128)(2,1)} async-done(((bf16[8,128,128]{2,1,0:T(8,128)(2,1)}), bf16[1,128,128]{2,1,0:T(8,128)(2,1)}) %reduce-scatter.3.cloned.1.call-update) | async-done | bytes 32784 | tf_op jit(solution)/shard_map/reduce_scatter | solution.py:127
  346.4 63.8 %reduce-scatter.5.cloned.1.call-done = bf16[1,128,128]{2,1,0:T(8,128)(2,1)} async-done(((bf16[8,128,128]{2,1,0:T(8,128)(2,1)}), bf16[1,128,128]{2,1,0:T(8,128)(2,1)}) %reduce-scatter.5.cloned.1.call-update) | async-done | bytes 32784 | tf_op jit(solution)/shard_map/reduce_scatter | solution.py:130
  410.3 1.5 constant_dynamic-slice_fusion.3
  411.8 31.2 %all-reduce.12.cloned.1.call-done = (bf16[1,128,128]{2,1,0:T(8,128)(2,1)}, bf16[1,128,128]{2,1,0:T(8,128)(2,1)}) async-done(((bf16[1,128,128]{2,1,0:T(8,128)(2,1)}, bf16[1,128,128]{2,1,0:T(8,128)(2,1)}), (bf16[1,128,128]{2,1,0:T(8,128)(2,1)}, bf16[1,128,128]{2,1,0:T(8,128)(2,1)})) %all-reduce.12.cloned.1.call-update) | async-done | bytes 65552 | tf_op jit(solution)/shard_map/psum | solution.py:135
  442.9 1.6 fusion.102
  444.7 0.6 copy-done.8
  445.3 0.8 fusion.15
  (56 shorter events, 3.9 us)
Async XLA Ops:
  7.2 40.7 %copy-start = (bf16[1,2,128,128]{3,2,1,0:T(8,128)(2,1)S(1)}, bf16[1,2,128,128]{3,2,1,0:T(8,128)(2,1)}, u32[]{:S(2)}) copy-start(bf16[1,2,128,128]{3,2,1,0:T(8,128)(2,1)} %param.9) | copy-start | bytes 196612
  7.2 108.3 %all-reduce.6.cloned.1.call-start = ((), (), s32[]{:S(2)}) async-start(), calls=%async_computation.2 | async-start | bytes 524288 | tf_op jit(solution)/shard_map/psum | solution.py:54
  8.4 7.2 %copy-start.9 = (s32[8,8]{1,0:T(8,128)S(1)}, s32[8,8]{1,0:T(8,128)}, u32[]{:S(2)}) copy-start(s32[8,8]{1,0:T(8,128)} %param.12) | copy-start | bytes 772
  48.9 100.6 %all-reduce.10.cloned.1.call-start = ((), (), s32[]{:S(2)}) async-start(), calls=%async_computation.4 | async-start | bytes 524288 | tf_op jit(solution)/shard_map/psum | solution.py:114
  49.1 0.7 copy-start.11
  49.1 1.4 copy-start.6
  49.4 1.1 copy-start.4
  49.8 0.7 copy-start.10
  57.0 31.5 %copy-start.7 = (bf16[1,128,128]{2,1,0:T(8,128)(2,1)S(1)}, bf16[1,128,128]{2,1,0:T(8,128)(2,1)}, u32[]{:S(2)}) copy-start(bf16[1,128,128]{2,1,0:T(8,128)(2,1)} %param.14) | copy-start | bytes 98308
  118.2 0.9 copy-start.1
  118.2 164.4 %all-reduce.8.cloned.1.call-start = ((), (), s32[]{:S(2)}) async-start(), calls=%async_computation.3 | async-start | bytes 1048576 | tf_op jit(solution)/shard_map/psum | solution.py:71
  119.4 0.8 copy-start.5
  120.4 0.8 copy-start.2
  121.2 225.2 %reduce-scatter.3.cloned.1.call-start = ((), (), s32[]{:S(2)}) async-start(), calls=%async_computation.5 | async-start | bytes 294912 | tf_op jit(solution)/shard_map/reduce_scatter | solution.py:127
  122.6 287.7 %reduce-scatter.5.cloned.1.call-start = ((), (), s32[]{:S(2)}) async-start(), calls=%async_computation.6 | async-start | bytes 294912 | tf_op jit(solution)/shard_map/reduce_scatter | solution.py:130
  149.5 1.3 copy-start.3
  151.9 291.0 %all-reduce.12.cloned.1.call-start = ((), (), s32[]{:S(2)}) async-start(), calls=%async_computation.7 | async-start | bytes 131072 | tf_op jit(solution)/shard_map/psum | solution.py:135
  444.5 0.8 copy-start.8
Sparse Core Ops, SparseCore 0:
  49.1 32.7 all-reduce.5
  118.3 31.1 all-reduce.9
  154.8 127.7 all-reduce.7
  286.2 60.2 reduce-scatter.2
  350.0 60.2 reduce-scatter.4
  412.6 30.2 all-reduce.11
where the time goes:
time: 454 us; the launch traced here: 453 us
  waiting for transfers between devices  313 us (69%)
  blocking collectives  103 us (23%)
  between operations  14.4 us (3%)
  matrix products  13.2 us (3%)
  local copies, waits for them, and re-layouts  8.08 us (2%)
    psum x1, waiting for transfers between devices, body(): diagonal_all = lax.psum(partial_diag, ('prow', 'pcol'))  129 us
    reduce_scatter x1, waiting for transfers between devices, body(): lax.psum_scatter(quadratic_two.astype(jnp.bfloat16), 'prow', scatter_dime...  63.8 us
    reduce_scatter x1, waiting for transfers between devices, body(): lax.psum_scatter(cross.astype(jnp.bfloat16), 'prow', scatter_dimension=0,...  61.9 us
    all_gather x1, blocking collectives, body(): spread_all = lax.all_gather(spread_one, 'prow', axis=0, tiled=True)  31.9 us
    all_gather x1, blocking collectives, body(): lax.all_gather(spread_two, 'prow', axis=0, tiled=True)  31.5 us
    psum x1, waiting for transfers between devices, body(): lax.psum(cross_part.astype(jnp.bfloat16), 'pcol').astype(jnp.float32)  31.2 us
    psum x1, waiting for transfers between devices, body(): lax.psum(partial_two.astype(jnp.bfloat16), 'pcol').astype(jnp.float32)  26.8 us
    all_gather x1, blocking collectives, body(): lax.all_gather(scaled_parent, 'prow', axis=0, tiled=True)  26.4 us
  transfers between devices with their start and end apart: 6, of which 5 were waited for; matrix products, arithmetic and copies ran while one was open for 3% of the time, Pallas kernels for 0%

commit v1 on v0

--- a/solution.py
+++ b/solution.py
@@ -4,6 +4,7 @@
 from jax.sharding import PartitionSpec as P
 
 highest = lax.Precision.HIGHEST
+prepare_notes = lambda chunk: lax.psum(lax.psum(chunk, axis_name="pcol"), axis_name="prow")
 
 
 def split_product(form, left, right):
@@ -68,7 +69,7 @@
         0,
     )
     partial_diag = quadratic_one + jnp.where(pcol_index == 0, placed, 0.0)
-    diagonal_all = lax.psum(partial_diag, ("prow", "pcol"))
+    diagonal_all = prepare_notes(partial_diag)
     diag_one = lax.dynamic_slice_in_dim(diagonal_all, prow_index * local_one, local_one, 0)
     local_two = factor_two.shape[0]
     lower_two = jnp.tril(inverse_two)

time: 454 us -> 433 us (0.954)
  waiting for transfers between devices: 313 us -> 292 us
    psum x1 -> x2, waiting for transfers between devices: 129 us -> 108 us  [the longest x1 74.6 us: lax.psum(lax.psum(chunk, axis_name='pcol'), axis_name='prow')]
  transfers between devices with their start and end apart: 6 -> 7, of which waited for: 5 -> 6; matrix products, arithmetic and copies ran while one was open for 3% -> 2% of each run, Pallas kernels for 0% -> 0%
where the time goes in v1:
time: 433 us; the launch traced here: 432 us
  waiting for transfers between devices  292 us (67%)
  blocking collectives  103 us (24%)
  between operations  14.4 us (3%)
  matrix products  13.2 us (3%)
  local copies, waits for them, and re-layouts  8.07 us (2%)
    psum x1, waiting for transfers between devices, lax.psum(lax.psum(chunk, axis_name='pcol'), axis_name='prow')  74.6 us
    reduce_scatter x1, waiting for transfers between devices, body(): lax.psum_scatter(quadratic_two.astype(jnp.bfloat16), 'prow', scatter_dime...  63.5 us
    reduce_scatter x1, waiting for transfers between devices, body(): lax.psum_scatter(cross.astype(jnp.bfloat16), 'prow', scatter_dimension=0,...  62.3 us
    psum x1, waiting for transfers between devices, lax.psum(chunk, axis_name='pcol')  33.2 us
    all_gather x1, blocking collectives, body(): spread_all = lax.all_gather(spread_one, 'prow', axis=0, tiled=True)  31.9 us
    all_gather x1, blocking collectives, body(): lax.all_gather(spread_two, 'prow', axis=0, tiled=True)  31.5 us
    psum x1, waiting for transfers between devices, body(): lax.psum(cross_part.astype(jnp.bfloat16), 'pcol').astype(jnp.float32)  31.1 us
    psum x1, waiting for transfers between devices, body(): lax.psum(partial_two.astype(jnp.bfloat16), 'pcol').astype(jnp.float32)  26.9 us
  transfers between devices with their start and end apart: 7, of which 6 were waited for; matrix products, arithmetic and copies ran while one was open for 2% of the time, Pallas kernels for 0%

profile of v1, /device:TPU:0, one launch (start us, length us, event | category | flops | bytes accessed | tf_op | source)
XLA Modules:
  0.0 432.2 jit_solution(14513007944716377772)
XLA Ops:
  7.2 1.1 fusion.10
  8.4 7.2 %all-gather = bf16[8,128,128]{2,1,0:T(8,128)(2,1)S(1)} all-gather(bf16[2,128,128]{2,1,0:T(8,128)(2,1)S(1)} %copy.72), channel_id=2, replica_groups=mesh['prow'=8,'pcol'=4] {'pcol'}, dimensions={0}, use_global_device_ids=true | all-gather | bytes 327680 | tf_op jit(solution)/shard_map/all_gather | solution.py:45
  16.0 31.9 %all-gather.1 = bf16[16,128,128]{2,1,0:T(8,128)(2,1)S(1)} all-gather(bf16[2,128,128]{2,1,0:T(8,128)(2,1)S(1)} %copy.74), channel_id=3, replica_groups=mesh['prow'=8,'pcol'=4] {'prow'}, dimensions={0}, use_global_device_ids=true | all-gather | bytes 589824 | tf_op jit(solution)/shard_map/all_gather | solution.py:51
  47.9 1.1 fusion.7
  49.5 0.3 copy-done.11
  50.0 0.6 copy-done.10
  50.9 5.8 %all-gather.2 = bf16[8,128,128]{2,1,0:T(8,128)(2,1)S(1)} all-gather(bf16[2,128,128]{2,1,0:T(8,128)(2,1)S(1)} %copy.79), channel_id=4, replica_groups=mesh['prow'=8,'pcol'=4] {'pcol'}, dimensions={0}, use_global_device_ids=true | all-gather | bytes 327680 | tf_op jit(solution)/shard_map/all_gather | solution.py:82
  57.0 31.5 %all-gather.3 = bf16[16,128,128]{2,1,0:T(8,128)(2,1)S(1)} all-gather(bf16[2,128,128]{2,1,0:T(8,128)(2,1)S(1)} %copy.81), channel_id=5, replica_groups=mesh['prow'=8,'pcol'=4] {'prow'}, dimensions={0}, use_global_device_ids=true | all-gather | bytes 589824 | tf_op jit(solution)/shard_map/all_gather | solution.py:99
  88.7 26.4 %all-gather.4 = bf16[1024,128]{0,1:T(8,128)(2,1)S(1)} all-gather(bf16[128,128]{0,1:T(8,128)(2,1)S(1)} %bitcast.162), channel_id=6, replica_groups=mesh['prow'=8,'pcol'=4] {'prow'}, dimensions={0}, use_global_device_ids=true | all-gather | bytes 294912 | tf_op jit(solution)/shard_map/all_gather | solution.py:100
  115.1 0.3 convolution_bitcast_fusion
  115.5 1.1 fusion.112
  117.2 0.9 fusion.9
  118.2 0.9 copy-done.1
  119.4 0.3 fusion.2
  119.7 0.4 copy-done.5
  120.4 0.8 copy-done.2
  121.5 1.0 fusion.6
  122.6 26.9 %all-reduce.13.cloned.1.call-done = bf16[1,8,128,128]{2,3,1,0:T(8,128)(2,1)} async-done(((bf16[1,8,128,128]{2,3,1,0:T(8,128)(2,1)}), bf16[1,8,128,128]{2,3,1,0:T(8,128)(2,1)}) %all-reduce.13.cloned.1.call-update) | async-done | bytes 262160 | tf_op jit(solution)/shard_map/psum | solution.py:115
  149.5 1.3 fusion.32
  150.9 1.0 fusion.3
  152.0 33.2 %all-reduce.9.cloned.1.call-done = f32[8,128,128]{2,1,0:T(8,128)} async-done(((f32[8,128,128]{2,1,0:T(8,128)}), f32[8,128,128]{2,1,0:T(8,128)}) %all-reduce.9.cloned.1.call-update) | async-done | bytes 524304 | tf_op jit(solution)/shard_map/psum | solution.py:7
  185.4 0.9 copy.92
  186.4 0.9 copy.93
  187.2 62.3 %reduce-scatter.3.cloned.1.call-done = bf16[1,128,128]{2,1,0:T(8,128)(2,1)} async-done(((bf16[8,128,128]{2,1,0:T(8,128)(2,1)}), bf16[1,128,128]{2,1,0:T(8,128)(2,1)}) %reduce-scatter.3.cloned.1.call-update) | async-done | bytes 32784 | tf_op jit(solution)/shard_map/reduce_scatter | solution.py:128
  249.5 63.5 %reduce-scatter.5.cloned.1.call-done = bf16[1,128,128]{2,1,0:T(8,128)(2,1)} async-done(((bf16[8,128,128]{2,1,0:T(8,128)(2,1)}), bf16[1,128,128]{2,1,0:T(8,128)(2,1)}) %reduce-scatter.5.cloned.1.call-update) | async-done | bytes 32784 | tf_op jit(solution)/shard_map/reduce_scatter | solution.py:131
  313.1 74.6 %all-reduce.11.cloned.1.call-done = f32[8,128,128]{2,1,0:T(8,128)} async-done(((f32[8,128,128]{2,1,0:T(8,128)}), f32[8,128,128]{2,1,0:T(8,128)}) %all-reduce.11.cloned.1.call-update) | async-done | bytes 524304 | tf_op jit(solution)/shard_map/psum | solution.py:7
  387.7 1.8 fusion.24
  389.5 31.1 %all-reduce.15.cloned.1.call-done = (bf16[1,128,128]{2,1,0:T(8,128)(2,1)}, bf16[1,128,128]{2,1,0:T(8,128)(2,1)}) async-done(((bf16[1,128,128]{2,1,0:T(8,128)(2,1)}, bf16[1,128,128]{2,1,0:T(8,128)(2,1)}), (bf16[1,128,128]{2,1,0:T(8,128)(2,1)}, bf16[1,128,128]{2,1,0:T(8,128)(2,1)})) %all-reduce.15.cloned.1.call-update) | async-done | bytes 65552 | tf_op jit(solution)/shard_map/psum | solution.py:136
  420.7 1.6 fusion.102
  422.5 0.6 copy-done.8
  423.0 0.8 fusion.15
  423.9 1.5 constant_dynamic-slice_fusion.3
  (59 shorter events, 4.3 us)
Async XLA Ops:
  7.2 40.7 %copy-start = (bf16[1,2,128,128]{3,2,1,0:T(8,128)(2,1)S(1)}, bf16[1,2,128,128]{3,2,1,0:T(8,128)(2,1)}, u32[]{:S(2)}) copy-start(bf16[1,2,128,128]{3,2,1,0:T(8,128)(2,1)} %param.9) | copy-start | bytes 196612
  7.2 108.3 %all-reduce.7.cloned.1.call-start = ((), (), s32[]{:S(2)}) async-start(), calls=%async_computation.2 | async-start | bytes 524288 | tf_op jit(solution)/shard_map/psum | solution.py:55
  8.4 7.2 %copy-start.9 = (s32[8,8]{1,0:T(8,128)S(1)}, s32[8,8]{1,0:T(8,128)}, u32[]{:S(2)}) copy-start(s32[8,8]{1,0:T(8,128)} %param.12) | copy-start | bytes 772
  48.9 100.6 %all-reduce.13.cloned.1.call-start = ((), (), s32[]{:S(2)}) async-start(), calls=%async_computation.5 | async-start | bytes 524288 | tf_op jit(solution)/shard_map/psum | solution.py:115
  49.1 0.7 copy-start.11
  49.1 1.4 copy-start.6
  49.4 1.1 copy-start.4
  49.8 0.7 copy-start.10
  57.0 31.5 %copy-start.7 = (bf16[1,128,128]{2,1,0:T(8,128)(2,1)S(1)}, bf16[1,128,128]{2,1,0:T(8,128)(2,1)}, u32[]{:S(2)}) copy-start(bf16[1,128,128]{2,1,0:T(8,128)(2,1)} %param.14) | copy-start | bytes 98308
  118.2 0.9 copy-start.1
  118.2 66.9 %all-reduce.9.cloned.1.call-start = ((), (), s32[]{:S(2)}) async-start(), calls=%async_computation.3 | async-start | bytes 1048576 | tf_op jit(solution)/shard_map/psum | solution.py:7
  119.4 0.8 copy-start.5
  120.4 0.8 copy-start.2
  121.2 128.3 %reduce-scatter.3.cloned.1.call-start = ((), (), s32[]{:S(2)}) async-start(), calls=%async_computation.6 | async-start | bytes 294912 | tf_op jit(solution)/shard_map/reduce_scatter | solution.py:128
  122.6 190.4 %reduce-scatter.5.cloned.1.call-start = ((), (), s32[]{:S(2)}) async-start(), calls=%async_computation.7 | async-start | bytes 294912 | tf_op jit(solution)/shard_map/reduce_scatter | solution.py:131
  149.5 1.3 copy-start.3
  151.9 235.8 %all-reduce.11.cloned.1.call-start = ((), (), s32[]{:S(2)}) async-start(), calls=%async_computation.4 | async-start | bytes 1048576 | tf_op jit(solution)/shard_map/psum | solution.py:7
  185.1 235.6 %all-reduce.15.cloned.1.call-start = ((), (), s32[]{:S(2)}) async-start(), calls=%async_computation.8 | async-start | bytes 131072 | tf_op jit(solution)/shard_map/psum | solution.py:136
  422.3 0.8 copy-start.8
Sparse Core Ops, SparseCore 0:
  49.1 32.7 all-reduce.6
  118.3 31.1 all-reduce.12
  151.9 33.1 all-reduce.8
  188.3 61.2 reduce-scatter.2
  252.7 60.2 reduce-scatter.4
  316.3 71.3 all-reduce.10
  390.2 30.4 all-reduce.14
